TPU v7x, 32 devices: a whole 2x2x4 slice. The times are simulated.
32 devices in a mesh: gx: 4 (over y, x), gy: 8 (over z, core).
Axes of the slice: x: 2, y: 2, z: 4, core: 2. Of those that a mesh axis runs over, the one named last changes fastest.
Arguments:
- start_block: bfloat16 [64, 65536], P(None, ('gx', 'gy')), may hold values from -200 to 200
- tiles: bfloat16 [256, 10, 256, 256], P(('gx', 'gy')), may hold values from -0.125 to 0.125
- tile_cols: int32 [256, 10], P(('gx', 'gy')), may hold values from 0 to 15, as said below
- send_rows: int32 [32, 2], P(('gx', 'gy')), may hold values from 0 to 7, as said below
- shifts: float32 [4], replicated, may hold values from -1 to 1
Outputs:
- basis_q: float32 [256, 65536], P(None, ('gx', 'gy'))
Inputs may be any that keep to these rules, and one draw needn't show every extreme that they name: `tile_cols`: every tile-row's first tile is its own diagonal tile; values below 8 name the partition's own tile-rows, the others ghost slots in the extended order. `send_rows`: each partition's 2 entries are distinct own tile-rows.
All inputs are finite; a program needn't handle non-finite values.
Results may differ from a plain program's by a relative error of at most 0.009.
The roundings to bfloat16 on the way count: a program that leaves them out, or rounds other values in their place, can miss the bound.
Values may be sent and summed in bfloat16 or wider, within the bound.
A program may use at most 64 MiB of HBM per device.

v0:
```python
import jax
import jax.numpy as jnp
from jax import lax
from jax.sharding import PartitionSpec as P


def extended_2(block, sides, width):
    for axis, dim in sides:
        count = lax.axis_size(axis)
        forward = [(i, i + 1) for i in range(count - 1)]
        backward = [(target, source) for source, target in forward]
        low = lax.ppermute(
            lax.slice_in_dim(block, block.shape[dim] - width, None, axis=dim), axis, forward
        )
        high = lax.ppermute(lax.slice_in_dim(block, 0, width, axis=dim), axis, backward)
        block = jnp.concatenate([low, block, high], axis=dim)
    return block


def apply_local(current, tiles, flat_cols, send_list):
    width = current.shape[0]
    tile_rows, slots, tile, _ = tiles.shape
    own = current.reshape(width, tile_rows, tile)
    outgoing = jnp.take(own, send_list, axis=1)
    framed = extended_2(outgoing[None, None], (("gx", 0), ("gy", 1)), 1)
    extended = jnp.concatenate(
        [own, framed[0, 1], framed[2, 1], framed[1, 0], framed[1, 2]], axis=1
    )
    picked = jnp.take(extended, flat_cols, axis=1).reshape(width, tile_rows, slots, tile)
    image = jnp.einsum("ctkb,tkab->cta", picked, tiles, preferred_element_type=jnp.float32)
    return image.reshape(width, tile_rows * tile)


def body(start_block, tiles, tile_cols, send_rows, shifts):
    flat_cols = tile_cols.reshape(-1)
    send_list = send_rows[0]
    current = start_block
    blocks = []
    for step in range(shifts.shape[0]):
        image = apply_local(current, tiles, flat_cols, send_list)
        current = (image - shifts[step] * current.astype(jnp.float32)).astype(jnp.bfloat16)
        blocks.append(current)
    basis = jnp.concatenate(blocks, axis=0)
    total_rows = basis.shape[1] * lax.axis_size("gx") * lax.axis_size("gy")
    local_gram = (
        lax.dot_general(basis, basis, (((1,), (1,)), ((), ())), preferred_element_type=jnp.float32)
        / total_rows
    )
    lower = jnp.linalg.cholesky(lax.psum(local_gram, ("gx", "gy")))
    return lax.linalg.triangular_solve(lower, basis.astype(jnp.float32), left_side=True, lower=True)


def solution(mesh):
    in_specs = (
        P(None, ("gx", "gy")),
        P(("gx", "gy"), None, None, None),
        P(("gx", "gy"), None),
        P(("gx", "gy"), None),
        P(),
    )
    out_specs = P(None, ("gx", "gy"))
    return jax.shard_map(body, mesh=mesh, in_specs=in_specs, out_specs=out_specs, check_vma=False)
```

profile of v0, /device:TPU:0, one launch (start us, length us, event | category | flops | bytes accessed | tf_op | source)
XLA Modules:
  0.0 325.0 jit_solution(11236422951529813700)
XLA Ops:
  9.5 1.3 collective-permute-start.1
  10.8 5.5 %collective-permute-start = (bf16[1,1,64,2,256]{4,2,3,1,0:T(8,128)(2,1)S(1)}, bf16[1,1,64,2,256]{4,2,3,1,0:T(8,128)(2,1)S(1)}, u32[]{:S(2)}, u32[]{:S(2)}) collective-permute-start(bf16[1,1,64,2,256]{4,2,3,1,0:T(8,128)(2,1)S(1)} %select_bitcast_fusion.3), channel_id=1, source_target_pairs={{0,8},{8,16},{16,24},{1,9},{9,17},{17,25},{2,10},{10,18},{18,26},{... | collective-permute-start | bytes 196616 | tf_op jit(solution)/shard_map/ppermute | solution.py:12
  18.0 1.5 fusion.28
  19.6 1.3 collective-permute-start.3
  20.9 3.0 collective-permute-start.2
  26.1 7.3 %convolution_bitcast_fusion.3 = f32[8,8,8,256]{3,2,1,0:T(8,128)S(1)} fusion(bf16[64,8,10,256]{3,0,2,1:T(8,128)(2,1)S(1)} %bitcast.176, bf16[8,10,256,256]{3,2,1,0:T(8,128)(2,1)} %param.10), kind=kOutput, calls=%fused_computation.19 | convolution fusion | flops 671088640 | bytes 13631488 | tf_op jit(solution)/shard_map/ctkb,tkab->cta/dot_general | solution.py:30
  34.7 1.3 collective-permute-start.5
  36.0 5.4 %collective-permute-start.4 = (bf16[1,1,64,2,256]{4,2,3,1,0:T(8,128)(2,1)S(1)}, bf16[1,1,64,2,256]{4,2,3,1,0:T(8,128)(2,1)S(1)}, u32[]{:S(2)}, u32[]{:S(2)}) collective-permute-start(bf16[1,1,64,2,256]{4,2,3,1,0:T(8,128)(2,1)S(1)} %select_bitcast_fusion.2), channel_id=1, source_target_pairs={{0,8},{8,16},{16,24},{1,9},{9,17},{17,25},{2,10},{10,18},{18,26},{... | collective-permute-start | bytes 196616 | tf_op jit(solution)/shard_map/ppermute | solution.py:12
  41.7 1.6 collective-permute-done.4
  43.4 1.3 collective-permute-start.7
  44.7 4.4 %collective-permute-start.6 = (bf16[3,1,64,2,256]{4,2,3,1,0:T(8,128)(2,1)S(1)}, bf16[3,1,64,2,256]{4,2,3,1,0:T(8,128)(2,1)S(1)}, u32[]{:S(2)}, u32[]{:S(2)}) collective-permute-start(bf16[3,1,64,2,256]{4,2,3,1,0:T(8,128)(2,1)S(1)} %pad_maximum_fusion.2), channel_id=1, source_target_pairs={{0,1},{1,2},{2,3},{3,4},{4,5},{5,6},{6,7},{8,9},{9,10},{10,11},{11... | collective-permute-start | bytes 589832 | tf_op jit(solution)/shard_map/ppermute | solution.py:12
  51.2 7.3 %convolution_bitcast_fusion.2 = f32[8,8,8,256]{3,2,1,0:T(8,128)S(1)} fusion(bf16[64,8,10,256]{3,0,2,1:T(8,128)(2,1)S(1)} %bitcast.177, bf16[8,10,256,256]{3,2,1,0:T(8,128)(2,1)} %param.10), kind=kOutput, calls=%fused_computation.18 | convolution fusion | flops 671088640 | bytes 13631488 | tf_op jit(solution)/shard_map/ctkb,tkab->cta/dot_general | solution.py:30
  59.9 1.3 collective-permute-start.9
  61.2 5.2 %collective-permute-start.8 = (bf16[1,1,64,2,256]{4,2,3,1,0:T(8,128)(2,1)S(1)}, bf16[1,1,64,2,256]{4,2,3,1,0:T(8,128)(2,1)S(1)}, u32[]{:S(2)}, u32[]{:S(2)}) collective-permute-start(bf16[1,1,64,2,256]{4,2,3,1,0:T(8,128)(2,1)S(1)} %select_bitcast_fusion.1), channel_id=1, source_target_pairs={{0,8},{8,16},{16,24},{1,9},{9,17},{17,25},{2,10},{10,18},{18,26},{... | collective-permute-start | bytes 196616 | tf_op jit(solution)/shard_map/ppermute | solution.py:12
  66.7 1.6 collective-permute-done.8
  68.3 1.3 collective-permute-start.11
  69.6 6.8 %collective-permute-start.10 = (bf16[3,1,64,2,256]{4,2,3,1,0:T(8,128)(2,1)S(1)}, bf16[3,1,64,2,256]{4,2,3,1,0:T(8,128)(2,1)S(1)}, u32[]{:S(2)}, u32[]{:S(2)}) collective-permute-start(bf16[3,1,64,2,256]{4,2,3,1,0:T(8,128)(2,1)S(1)} %pad_maximum_fusion.3), channel_id=1, source_target_pairs={{0,1},{1,2},{2,3},{3,4},{4,5},{5,6},{6,7},{8,9},{9,10},{10,11},{11... | collective-permute-start | bytes 589832 | tf_op jit(solution)/shard_map/ppermute | solution.py:12
  78.7 7.3 %convolution_bitcast_fusion.1 = f32[8,8,8,256]{3,2,1,0:T(8,128)S(1)} fusion(bf16[64,8,10,256]{3,0,2,1:T(8,128)(2,1)S(1)} %bitcast.178, bf16[8,10,256,256]{3,2,1,0:T(8,128)(2,1)} %param.10), kind=kOutput, calls=%fused_computation.17 | convolution fusion | flops 671088640 | bytes 13631488 | tf_op jit(solution)/shard_map/ctkb,tkab->cta/dot_general | solution.py:30
  88.7 5.8 %collective-permute-start.12 = (bf16[1,1,64,2,256]{4,2,3,1,0:T(8,128)(2,1)S(1)}, bf16[1,1,64,2,256]{4,2,3,1,0:T(8,128)(2,1)S(1)}, u32[]{:S(2)}, u32[]{:S(2)}) collective-permute-start(bf16[1,1,64,2,256]{4,2,3,1,0:T(8,128)(2,1)S(1)} %select_bitcast_fusion), channel_id=1, source_target_pairs={{0,8},{8,16},{16,24},{1,9},{9,17},{17,25},{2,10},{10,18},{18,26},{... | collective-permute-start | bytes 196616 | tf_op jit(solution)/shard_map/ppermute | solution.py:12
  94.8 1.6 collective-permute-done.12
  96.4 1.3 collective-permute-start.15
  97.7 6.8 %collective-permute-start.14 = (bf16[3,1,64,2,256]{4,2,3,1,0:T(8,128)(2,1)S(1)}, bf16[3,1,64,2,256]{4,2,3,1,0:T(8,128)(2,1)S(1)}, u32[]{:S(2)}, u32[]{:S(2)}) collective-permute-start(bf16[3,1,64,2,256]{4,2,3,1,0:T(8,128)(2,1)S(1)} %pad_maximum_fusion.4), channel_id=1, source_target_pairs={{0,1},{1,2},{2,3},{3,4},{4,5},{5,6},{6,7},{8,9},{9,10},{10,11},{11... | collective-permute-start | bytes 589832 | tf_op jit(solution)/shard_map/ppermute | solution.py:12
  106.5 7.3 %convolution_bitcast_fusion = f32[8,8,8,256]{3,2,1,0:T(8,128)S(1)} fusion(bf16[64,8,10,256]{3,0,2,1:T(8,128)(2,1)S(1)} %bitcast.175, bf16[8,10,256,256]{3,2,1,0:T(8,128)(2,1)} %param.10), kind=kOutput, calls=%fused_computation.16 | convolution fusion | flops 671088640 | bytes 13631488 | tf_op jit(solution)/shard_map/ctkb,tkab->cta/dot_general | solution.py:30
  115.8 136.7 %all-reduce.3.cloned.1.call-done = f32[256,256]{0,1:T(8,128)} async-done(((f32[256,256]{0,1:T(8,128)}), f32[256,256]{0,1:T(8,128)}) %all-reduce.3.cloned.1.call-update) | async-done | bytes 262160 | tf_op jit(solution)/shard_map/psum | solution.py:49
  254.6 11.7 %cholesky.50 = f32[128,128]{1,0:T(8,128)S(1)} custom-call(f32[128,128]{1,0:T(8,128)S(1)} %cholesky.118), custom_call_target="Cholesky" | custom-call | tf_op jit(solution)/shard_map/jit(cholesky)/cholesky | solution.py:49
  266.4 9.8 %custom-call.14 = f32[1,128,128]{1,2,0:T(8,128)S(1)} custom-call(f32[1,128,128]{2,1,0:T(8,128)S(1)} %get-tuple-element.28), custom_call_target="InvertDiagBlocksLowerTriangular" | custom-call | tf_op jit(solution)/shard_map/jit(cholesky)/cholesky | solution.py:49
  276.7 11.9 %cholesky.105 = f32[128,128]{1,0:T(8,128)S(1)} custom-call(f32[128,128]{1,0:T(8,128)S(1)} %convolution_subtract_fusion.1), custom_call_target="Cholesky" | custom-call | tf_op jit(solution)/shard_map/jit(cholesky)/cholesky | solution.py:49
  290.5 3.8 %while.1 = (s32[]{:T(128)}, f32[256,256]{1,0:T(8,128)S(1)}, s32[2,2]{1,0:T(2,128)S(1)}, f32[2,128,128]{2,1,0:T(8,128)S(1)}, s32[]{:T(128)}) while((s32[]{:T(128)}, f32[256,256]{1,0:T(8,128)S(1)}, s32[2,2]{1,0:T(2,128)S(1)}, f32[2,128,128]{2,1,0:T(8,128)S(1)}, s32[]{:T(128)}) %tuple.28), condition=%wide.while_cond, body=%wide.while_body.sunk | while | flops 2 | bytes 131189 | solution.py:50
  291.1 1.3 bitcast_dynamic-update-slice_fusion.10
  293.0 1.3 bitcast_dynamic-update-slice_fusion.10
  294.3 19.7 %custom-call.15 = f32[2,128,128]{1,2,0:T(8,128)S(1)} custom-call(f32[2,128,128]{2,1,0:T(8,128)S(1)} %get-tuple-element.14), custom_call_target="InvertDiagBlocksLowerTriangular" | custom-call | tf_op jit(solution)/shard_map/triangular_solve | solution.py:50
  316.7 1.5 pad_maximum_fusion
  (108 shorter events, 28.6 us)
Async XLA Ops:
  6.5 246.0 %all-reduce.3.cloned.1.call-start = ((), (), s32[]{:S(2)}) async-start(), calls=%async_computation | async-start | bytes 524288 | tf_op jit(solution)/shard_map/psum | solution.py:49
  9.5 10.0 %collective-permute-start.1 = (bf16[1,1,64,2,256]{4,2,3,1,0:T(8,128)(2,1)S(1)}, bf16[1,1,64,2,256]{4,2,3,1,0:T(8,128)(2,1)S(1)}, u32[]{:S(2)}, u32[]{:S(2)}) collective-permute-start(bf16[1,1,64,2,256]{4,2,3,1,0:T(8,128)(2,1)S(1)} %select_bitcast_fusion.3), channel_id=1, source_target_pairs={{8,0},{16,8},{24,16},{9,1},{17,9},{25,17},{10,2},{18,10},{26,18},{... | collective-permute-start | bytes 196616 | tf_op jit(solution)/shard_map/ppermute | solution.py:15
  10.8 8.8 %collective-permute-start = (bf16[1,1,64,2,256]{4,2,3,1,0:T(8,128)(2,1)S(1)}, bf16[1,1,64,2,256]{4,2,3,1,0:T(8,128)(2,1)S(1)}, u32[]{:S(2)}, u32[]{:S(2)}) collective-permute-start(bf16[1,1,64,2,256]{4,2,3,1,0:T(8,128)(2,1)S(1)} %select_bitcast_fusion.3), channel_id=1, source_target_pairs={{0,8},{8,16},{16,24},{1,9},{9,17},{17,25},{2,10},{10,18},{18,26},{... | collective-permute-start | bytes 196616 | tf_op jit(solution)/shard_map/ppermute | solution.py:12
  19.6 5.4 %collective-permute-start.3 = (bf16[3,1,64,2,256]{4,2,3,1,0:T(8,128)(2,1)S(1)}, bf16[3,1,64,2,256]{4,2,3,1,0:T(8,128)(2,1)S(1)}, u32[]{:S(2)}, u32[]{:S(2)}) collective-permute-start(bf16[3,1,64,2,256]{4,2,3,1,0:T(8,128)(2,1)S(1)} %pad_maximum_fusion.1), channel_id=1, source_target_pairs={{1,0},{2,1},{3,2},{4,3},{5,4},{6,5},{7,6},{9,8},{10,9},{11,10},{12... | collective-permute-start | bytes 589832 | tf_op jit(solution)/shard_map/ppermute | solution.py:15
  20.9 4.1 %collective-permute-start.2 = (bf16[3,1,64,2,256]{4,2,3,1,0:T(8,128)(2,1)S(1)}, bf16[3,1,64,2,256]{4,2,3,1,0:T(8,128)(2,1)S(1)}, u32[]{:S(2)}, u32[]{:S(2)}) collective-permute-start(bf16[3,1,64,2,256]{4,2,3,1,0:T(8,128)(2,1)S(1)} %pad_maximum_fusion.1), channel_id=1, source_target_pairs={{0,1},{1,2},{2,3},{3,4},{4,5},{5,6},{6,7},{8,9},{9,10},{10,11},{11... | collective-permute-start | bytes 589832 | tf_op jit(solution)/shard_map/ppermute | solution.py:12
  26.1 7.3 %copy-start.5 = (bf16[64,2048]{1,0:T(8,128)(2,1)S(1)}, bf16[64,2048]{1,0:T(8,128)(2,1)}, u32[]{:S(2)}) copy-start(bf16[64,2048]{1,0:T(8,128)(2,1)} %param.9) | copy-start | bytes 786436
  34.7 7.0 %collective-permute-start.5 = (bf16[1,1,64,2,256]{4,2,3,1,0:T(8,128)(2,1)S(1)}, bf16[1,1,64,2,256]{4,2,3,1,0:T(8,128)(2,1)S(1)}, u32[]{:S(2)}, u32[]{:S(2)}) collective-permute-start(bf16[1,1,64,2,256]{4,2,3,1,0:T(8,128)(2,1)S(1)} %select_bitcast_fusion.2), channel_id=1, source_target_pairs={{8,0},{16,8},{24,16},{9,1},{17,9},{25,17},{10,2},{18,10},{26,18},{... | collective-permute-start | bytes 196616 | tf_op jit(solution)/shard_map/ppermute | solution.py:15
  36.0 7.3 %collective-permute-start.4 = (bf16[1,1,64,2,256]{4,2,3,1,0:T(8,128)(2,1)S(1)}, bf16[1,1,64,2,256]{4,2,3,1,0:T(8,128)(2,1)S(1)}, u32[]{:S(2)}, u32[]{:S(2)}) collective-permute-start(bf16[1,1,64,2,256]{4,2,3,1,0:T(8,128)(2,1)S(1)} %select_bitcast_fusion.2), channel_id=1, source_target_pairs={{0,8},{8,16},{16,24},{1,9},{9,17},{17,25},{2,10},{10,18},{18,26},{... | collective-permute-start | bytes 196616 | tf_op jit(solution)/shard_map/ppermute | solution.py:12
  43.4 6.8 %collective-permute-start.7 = (bf16[3,1,64,2,256]{4,2,3,1,0:T(8,128)(2,1)S(1)}, bf16[3,1,64,2,256]{4,2,3,1,0:T(8,128)(2,1)S(1)}, u32[]{:S(2)}, u32[]{:S(2)}) collective-permute-start(bf16[3,1,64,2,256]{4,2,3,1,0:T(8,128)(2,1)S(1)} %pad_maximum_fusion.2), channel_id=1, source_target_pairs={{1,0},{2,1},{3,2},{4,3},{5,4},{6,5},{7,6},{9,8},{10,9},{11,10},{12... | collective-permute-start | bytes 589832 | tf_op jit(solution)/shard_map/ppermute | solution.py:15
  44.7 5.5 %collective-permute-start.6 = (bf16[3,1,64,2,256]{4,2,3,1,0:T(8,128)(2,1)S(1)}, bf16[3,1,64,2,256]{4,2,3,1,0:T(8,128)(2,1)S(1)}, u32[]{:S(2)}, u32[]{:S(2)}) collective-permute-start(bf16[3,1,64,2,256]{4,2,3,1,0:T(8,128)(2,1)S(1)} %pad_maximum_fusion.2), channel_id=1, source_target_pairs={{0,1},{1,2},{2,3},{3,4},{4,5},{5,6},{6,7},{8,9},{9,10},{10,11},{11... | collective-permute-start | bytes 589832 | tf_op jit(solution)/shard_map/ppermute | solution.py:12
  59.3 18.3 %copy-start = (bf16[64,2048]{1,0:T(8,128)(2,1)}, bf16[64,2048]{1,0:T(8,128)(2,1)S(1)}, u32[]{:S(2)}) copy-start(bf16[64,2048]{1,0:T(8,128)(2,1)S(1)} %subtract_convert_fusion.2) | copy-start | bytes 786436
  59.9 6.8 %collective-permute-start.9 = (bf16[1,1,64,2,256]{4,2,3,1,0:T(8,128)(2,1)S(1)}, bf16[1,1,64,2,256]{4,2,3,1,0:T(8,128)(2,1)S(1)}, u32[]{:S(2)}, u32[]{:S(2)}) collective-permute-start(bf16[1,1,64,2,256]{4,2,3,1,0:T(8,128)(2,1)S(1)} %select_bitcast_fusion.1), channel_id=1, source_target_pairs={{8,0},{16,8},{24,16},{9,1},{17,9},{25,17},{10,2},{18,10},{26,18},{... | collective-permute-start | bytes 196616 | tf_op jit(solution)/shard_map/ppermute | solution.py:15
  61.2 7.1 %collective-permute-start.8 = (bf16[1,1,64,2,256]{4,2,3,1,0:T(8,128)(2,1)S(1)}, bf16[1,1,64,2,256]{4,2,3,1,0:T(8,128)(2,1)S(1)}, u32[]{:S(2)}, u32[]{:S(2)}) collective-permute-start(bf16[1,1,64,2,256]{4,2,3,1,0:T(8,128)(2,1)S(1)} %select_bitcast_fusion.1), channel_id=1, source_target_pairs={{0,8},{8,16},{16,24},{1,9},{9,17},{17,25},{2,10},{10,18},{18,26},{... | collective-permute-start | bytes 196616 | tf_op jit(solution)/shard_map/ppermute | solution.py:12
  68.3 9.2 %collective-permute-start.11 = (bf16[3,1,64,2,256]{4,2,3,1,0:T(8,128)(2,1)S(1)}, bf16[3,1,64,2,256]{4,2,3,1,0:T(8,128)(2,1)S(1)}, u32[]{:S(2)}, u32[]{:S(2)}) collective-permute-start(bf16[3,1,64,2,256]{4,2,3,1,0:T(8,128)(2,1)S(1)} %pad_maximum_fusion.3), channel_id=1, source_target_pairs={{1,0},{2,1},{3,2},{4,3},{5,4},{6,5},{7,6},{9,8},{10,9},{11,10},{12... | collective-permute-start | bytes 589832 | tf_op jit(solution)/shard_map/ppermute | solution.py:15
  69.6 7.9 %collective-permute-start.10 = (bf16[3,1,64,2,256]{4,2,3,1,0:T(8,128)(2,1)S(1)}, bf16[3,1,64,2,256]{4,2,3,1,0:T(8,128)(2,1)S(1)}, u32[]{:S(2)}, u32[]{:S(2)}) collective-permute-start(bf16[3,1,64,2,256]{4,2,3,1,0:T(8,128)(2,1)S(1)} %pad_maximum_fusion.3), channel_id=1, source_target_pairs={{0,1},{1,2},{2,3},{3,4},{4,5},{5,6},{6,7},{8,9},{9,10},{10,11},{11... | collective-permute-start | bytes 589832 | tf_op jit(solution)/shard_map/ppermute | solution.py:12
  78.6 7.3 %copy-start.1 = (bf16[64,2048]{1,0:T(8,128)(2,1)S(1)}, bf16[64,2048]{1,0:T(8,128)(2,1)}, u32[]{:S(2)}) copy-start(bf16[64,2048]{1,0:T(8,128)(2,1)} %copy-done) | copy-start | bytes 786436
  86.8 18.6 %copy-start.3 = (bf16[64,2048]{1,0:T(8,128)(2,1)}, bf16[64,2048]{1,0:T(8,128)(2,1)S(1)}, u32[]{:S(2)}) copy-start(bf16[64,2048]{1,0:T(8,128)(2,1)S(1)} %subtract_convert_fusion.1) | copy-start | bytes 786436
  87.4 7.4 %collective-permute-start.13 = (bf16[1,1,64,2,256]{4,2,3,1,0:T(8,128)(2,1)S(1)}, bf16[1,1,64,2,256]{4,2,3,1,0:T(8,128)(2,1)S(1)}, u32[]{:S(2)}, u32[]{:S(2)}) collective-permute-start(bf16[1,1,64,2,256]{4,2,3,1,0:T(8,128)(2,1)S(1)} %select_bitcast_fusion), channel_id=1, source_target_pairs={{8,0},{16,8},{24,16},{9,1},{17,9},{25,17},{10,2},{18,10},{26,18},{... | collective-permute-start | bytes 196616 | tf_op jit(solution)/shard_map/ppermute | solution.py:15
  88.7 7.7 %collective-permute-start.12 = (bf16[1,1,64,2,256]{4,2,3,1,0:T(8,128)(2,1)S(1)}, bf16[1,1,64,2,256]{4,2,3,1,0:T(8,128)(2,1)S(1)}, u32[]{:S(2)}, u32[]{:S(2)}) collective-permute-start(bf16[1,1,64,2,256]{4,2,3,1,0:T(8,128)(2,1)S(1)} %select_bitcast_fusion), channel_id=1, source_target_pairs={{0,8},{8,16},{16,24},{1,9},{9,17},{17,25},{2,10},{10,18},{18,26},{... | collective-permute-start | bytes 196616 | tf_op jit(solution)/shard_map/ppermute | solution.py:12
  96.4 8.9 %collective-permute-start.15 = (bf16[3,1,64,2,256]{4,2,3,1,0:T(8,128)(2,1)S(1)}, bf16[3,1,64,2,256]{4,2,3,1,0:T(8,128)(2,1)S(1)}, u32[]{:S(2)}, u32[]{:S(2)}) collective-permute-start(bf16[3,1,64,2,256]{4,2,3,1,0:T(8,128)(2,1)S(1)} %pad_maximum_fusion.4), channel_id=1, source_target_pairs={{1,0},{2,1},{3,2},{4,3},{5,4},{6,5},{7,6},{9,8},{10,9},{11,10},{12... | collective-permute-start | bytes 589832 | tf_op jit(solution)/shard_map/ppermute | solution.py:15
  97.7 7.6 %collective-permute-start.14 = (bf16[3,1,64,2,256]{4,2,3,1,0:T(8,128)(2,1)S(1)}, bf16[3,1,64,2,256]{4,2,3,1,0:T(8,128)(2,1)S(1)}, u32[]{:S(2)}, u32[]{:S(2)}) collective-permute-start(bf16[3,1,64,2,256]{4,2,3,1,0:T(8,128)(2,1)S(1)} %pad_maximum_fusion.4), channel_id=1, source_target_pairs={{0,1},{1,2},{2,3},{3,4},{4,5},{5,6},{6,7},{8,9},{9,10},{10,11},{11... | collective-permute-start | bytes 589832 | tf_op jit(solution)/shard_map/ppermute | solution.py:12
  106.5 7.4 %copy-start.4 = (bf16[64,2048]{1,0:T(8,128)(2,1)S(1)}, bf16[64,2048]{1,0:T(8,128)(2,1)}, u32[]{:S(2)}) copy-start(bf16[64,2048]{1,0:T(8,128)(2,1)} %copy-done.3) | copy-start | bytes 786436
  106.5 8.1 %copy-start.2 = (bf16[64,2048]{1,0:T(8,128)(2,1)S(1)}, bf16[64,2048]{1,0:T(8,128)(2,1)}, u32[]{:S(2)}) copy-start(bf16[64,2048]{1,0:T(8,128)(2,1)} %copy-done) | copy-start | bytes 786436
Sparse Core Ops, SparseCore 0:
  115.9 136.5 all-reduce.2
where the time goes:
time: 326 us; the launch traced here: 325 us
  waiting for transfers between devices  146 us (45%)
  other arithmetic  62.1 us (19%)
  starting transfers between devices  53.3 us (16%)
  matrix products  33.4 us (10%)
  between operations  15.3 us (5%)
  local copies, waits for them, and re-layouts  14.7 us (5%)
    psum x1, waiting for transfers between devices, body(): lower = jnp.linalg.cholesky(lax.psum(local_gram, ('gx', 'gy')))  137 us
    ppermute x8, starting transfers between devices, extended_2(): lax.ppermute(lax.slice_in_dim(block, block.shape[dim] - width, None, axis...  43 us
    another operation x6, other arithmetic, body(): lower = jnp.linalg.cholesky(lax.psum(local_gram, ('gx', 'gy')))  34.1 us
    dot_general x4, matrix products, apply_local(): jnp.einsum('ctkb,tkab->cta', picked, tiles, preferred_element_type=jnp.fl...  29.1 us
    another operation x4, other arithmetic, body(): lax.linalg.triangular_solve(lower, basis.astype(jnp.float32), left_side=T...  21.2 us
    ppermute x8, starting transfers between devices, extended_2(): lax.ppermute(lax.slice_in_dim(block, 0, width, axis=dim), axis, backward)  10.3 us
    ppermute x8, waiting for transfers between devices, extended_2(): lax.ppermute(lax.slice_in_dim(block, block.shape[dim] - width, None, axis...  8.61 us
  transfers between devices with their start and end apart: 17, of which 11 were waited for; matrix products, arithmetic and copies ran while one was open for 1% of the time, Pallas kernels for 0%

commit v1 on v0

v1 whole, which is shorter than its diff:
```python
import functools

import jax
import jax.numpy as jnp
from jax import lax
from jax.experimental import pallas as pl
from jax.experimental.pallas import tpu as pltpu
from jax.sharding import PartitionSpec as P

MESH = pl.DeviceIdType.MESH
F32 = jnp.float32
BF16 = jnp.bfloat16
NT_DIMS = (((1,), (1,)), ((), ()))


def nt(a, b, precision=None):
    return lax.dot_general(a, b, NT_DIMS, precision=precision, preferred_element_type=F32)


def krylov_kernel(dims, send_rows, tile_cols, shifts, start, tiles_hbm, basis, gram, *scratch):
    nx, ny, steps, tile_rows, slots, ghosts, tile, width, total = dims
    tiles, tile_sem = scratch[0:2]
    halo_send, halo_recv, rs_send, rs_recv, xs_send, xs_recv, ag_send, ag_recv = scratch[2:10]
    at = 10
    ext = scratch[at:at + steps]
    outbox = scratch[at + steps:at + 2 * steps]
    part = scratch[at + 2 * steps:at + 3 * steps]
    rs = scratch[at + 3 * steps:at + 4 * steps]
    xs = scratch[at + 4 * steps:at + 5 * steps]
    full = scratch[at + 5 * steps:at + 6 * steps]
    first = scratch[at + 6 * steps]
    piece = width // ny
    ix, iy = lax.axis_index("gx"), lax.axis_index("gy")

    def tile_copy(t):
        return pltpu.make_async_copy(tiles_hbm.at[t], tiles.at[t], tile_sem.at[t])

    for t in range(tile_rows):
        tile_copy(t).start()

    for s in range(steps):
        ext[s][tile_rows:] = jnp.zeros(ext[s][tile_rows:].shape, BF16)

    barrier = pltpu.get_barrier_semaphore()

    def greet_y(d, c):
        pl.semaphore_signal(barrier, inc=1, device_id=(ix, lax.rem(iy + d, ny)), device_id_type=MESH)
        return c

    def greet_x(d, c):
        pl.semaphore_signal(barrier, inc=1, device_id=(lax.rem(ix + d, nx), iy), device_id_type=MESH)
        return c

    lax.fori_loop(1, ny, greet_y, 0)
    lax.fori_loop(1, nx, greet_x, 0)

    for t in range(tile_rows):
        rows = start[:, t * tile:(t + 1) * tile]
        ext[0][t] = rows
        first[t] = rows
    for s in range(ghosts):
        outbox[0][s] = first[send_rows[0, s]]
    for j in range(0, steps, 2):
        if j + 1 < steps:
            basis[(j + 1) * width:(j + 2) * width, :] = jnp.zeros((width, basis.shape[1]), BF16)
    pl.semaphore_wait(barrier, nx + ny - 2)

    def halo(j):
        out = []
        sides = (
            (ix < nx - 1, ix > 0, (ix + 1, iy)),
            (ix > 0, ix < nx - 1, (ix - 1, iy)),
            (iy < ny - 1, iy > 0, (ix, iy + 1)),
            (iy > 0, iy < ny - 1, (ix, iy - 1)),
        )
        for n, (sends, receives, peer) in enumerate(sides):
            low = tile_rows + n * ghosts
            copy = pltpu.make_async_remote_copy(
                src_ref=outbox[j], dst_ref=ext[j].at[low:low + ghosts],
                send_sem=halo_send.at[j, n], recv_sem=halo_recv.at[j, n],
                device_id=peer, device_id_type=MESH)
            out.append((sends, receives, copy))
        return out

    def halo_start(j):
        for sends, _, copy in halo(j):
            pl.when(sends)(copy.start)

    def halo_wait(j):
        for _, receives, copy in halo(j):
            pl.when(receives)(copy.wait_recv)

    def halo_drain(j):
        for sends, _, copy in halo(j):
            pl.when(sends)(copy.wait_send)

    def rs_copy(u, d):
        peer = lax.rem(iy + d, ny)
        return pltpu.make_async_remote_copy(
            src_ref=part[u].at[peer], dst_ref=rs[u].at[d],
            send_sem=rs_send.at[u, d], recv_sem=rs_recv.at[u, d],
            device_id=(ix, peer), device_id_type=MESH)

    def xs_copy(u, d):
        return pltpu.make_async_remote_copy(
            src_ref=xs[u].at[0], dst_ref=xs[u].at[d],
            send_sem=xs_send.at[u, d], recv_sem=xs_recv.at[u, d],
            device_id=(lax.rem(ix + d, nx), iy), device_id_type=MESH)

    def ag_copy(u, d):
        return pltpu.make_async_remote_copy(
            src_ref=full[u].at[iy], dst_ref=full[u].at[iy],
            send_sem=ag_send.at[u, d], recv_sem=ag_recv.at[u, d],
            device_id=(ix, lax.rem(iy + d, ny)), device_id_type=MESH)

    def each(count, act):
        def turn(d, c):
            act(d)
            return c
        lax.fori_loop(1, count, turn, 0)

    def phase_1(u):
        each(ny, lambda d: rs_copy(u, d).start())

    def phase_2(u):
        each(ny, lambda d: rs_copy(u, d).wait_recv())
        total_piece = part[u][iy]
        for d in range(1, ny):
            total_piece = total_piece + rs[u][d]
        xs[u][0] = total_piece
        each(nx, lambda d: xs_copy(u, d).start())

    def phase_3(u):
        each(nx, lambda d: xs_copy(u, d).wait_recv())
        total_piece = xs[u][lax.rem(ix, nx)]
        for source in range(1, nx):
            total_piece = total_piece + xs[u][lax.rem(ix - source + nx, nx)]
        full[u][iy] = total_piece
        each(ny, lambda d: ag_copy(u, d).start())

    def phase_4(u):
        each(ny, lambda d: ag_copy(u, d).wait_recv())
        for p in range(ny):
            low = u * width + p * piece
            gram[low:low + piece, :full[u].shape[2]] = full[u][p]

    def drain(u):
        each(ny, lambda d: rs_copy(u, d).wait_send())
        each(nx, lambda d: xs_copy(u, d).wait_send())
        each(ny, lambda d: ag_copy(u, d).wait_send())

    def row_image(j, r):
        acc = nt(ext[j][tile_cols[r, 0]], tiles[r, 0])
        for k in range(1, slots):
            acc = acc + nt(ext[j][tile_cols[r, k]], tiles[r, k])
        return (acc - shifts[j] * ext[j][r].astype(F32)).astype(BF16)

    halo_start(0)
    for t in range(tile_rows):
        tile_copy(t).wait()

    for j in range(steps):
        halo_wait(j)
        if j + 1 < steps:
            for s in range(ghosts):
                outbox[j + 1][s] = row_image(j, send_rows[0, s])
            halo_start(j + 1)

        def row(t, c):
            value = row_image(j, t)
            if j + 1 < steps:
                ext[j + 1][t] = value
            basis[j * width:(j + 1) * width, pl.ds(pl.multiple_of(t * tile, tile), tile)] = value
            return c

        lax.fori_loop(0, tile_rows, row, 0)
        local = nt(basis[j * width:(j + 1) * width, :], basis[0:part[j].shape[2], :]) / total
        for p in range(ny):
            part[j][p] = local[p * piece:(p + 1) * piece]
        phase_1(j)
        if j >= 1:
            phase_2(j - 1)
        if j >= 2:
            phase_3(j - 2)

    last = steps - 1
    phase_2(last)
    if steps > 1:
        phase_3(last - 1)
    phase_3(last)
    for u in range(steps):
        phase_4(u)
    for u in range(steps):
        halo_drain(u)
        drain(u)


def finish_kernel(dims, basis, gram, out, inverse, staged, sem):
    steps, width, chunk = dims
    high = lax.Precision.HIGHEST
    size = steps * width
    inverse[...] = jnp.zeros((size, size), F32)
    rows = lax.broadcasted_iota(jnp.int32, (8, 2 * width), 0)
    eye_r = lax.broadcasted_iota(jnp.int32, (width, width), 0)
    eye_c = lax.broadcasted_iota(jnp.int32, (width, width), 1)
    eye = jnp.where(eye_r == eye_c, 1.0, 0.0).astype(F32)
    for j in range(steps):
        lo, hi = j * width, (j + 1) * width
        block = gram[lo:hi, lo:hi]
        if j:
            previous = inverse[0:lo, 0:lo]
            left = nt(gram[lo:hi, 0:lo], previous, high)
            block = block - nt(left, left, high)
        work = jnp.concatenate([block, eye], axis=1)
        groups = [work[g * 8:(g + 1) * 8] for g in range(width // 8)]
        done = []
        for k in range(width):
            g, r = k // 8, k % 8
            pivot_row = groups[g][r:r + 1]
            pivot = groups[g][r:r + 1, k:k + 1]
            done.append(pivot_row * lax.rsqrt(pivot))
            scaled = pivot_row / pivot
            for h in range(g, width // 8):
                update = groups[h] - groups[h][:, k:k + 1] * scaled
                groups[h] = jnp.where(rows > r, update, groups[h]) if h == g else update
        own = jnp.concatenate(done, axis=0)[:, width:]
        inverse[lo:hi, lo:hi] = own
        if j:
            cross = jnp.dot(left, previous, precision=high, preferred_element_type=F32)
            inverse[lo:hi, 0:lo] = -jnp.dot(own, cross, precision=high, preferred_element_type=F32)
    whole = inverse[...]
    main = whole.astype(BF16)
    rest = (whole - main.astype(F32)).astype(BF16)
    copies = []
    for n in range(basis.shape[1] // chunk):
        cols = slice(n * chunk, (n + 1) * chunk)
        b = basis[:, cols]
        staged[:, cols] = jnp.dot(main, b, preferred_element_type=F32) + jnp.dot(
            rest, b, preferred_element_type=F32)
        copy = pltpu.make_async_copy(staged.at[:, cols], out.at[:, cols], sem.at[n])
        copy.start()
        copies.append(copy)
    for copy in copies:
        copy.wait()


def body(nx, ny, start_block, tiles, tile_cols, send_rows, shifts):
    width, nodes = start_block.shape
    tile_rows, slots, tile, _ = tiles.shape
    ghosts = send_rows.shape[1]
    steps = shifts.shape[0]
    size = steps * width
    piece = width // ny
    dims = (nx, ny, steps, tile_rows, slots, ghosts, tile, width, nodes * nx * ny)
    spans = [-(-(u + 1) * width // 128) * 128 for u in range(steps)]
    dma = pltpu.SemaphoreType.DMA
    vmem = pl.BlockSpec(memory_space=pltpu.VMEM)
    smem = pl.BlockSpec(memory_space=pltpu.SMEM)
    basis, gram = pl.pallas_call(
        functools.partial(krylov_kernel, dims),
        out_shape=(
            jax.ShapeDtypeStruct((size, nodes), BF16),
            jax.ShapeDtypeStruct((size, size), F32),
        ),
        in_specs=[smem, smem, smem, vmem, pl.BlockSpec(memory_space=pl.ANY)],
        out_specs=(vmem, vmem),
        scratch_shapes=[
            pltpu.VMEM(tiles.shape, BF16),
            dma((tile_rows,)),
            dma((steps, 4)), dma((steps, 4)),
            dma((steps, ny)), dma((steps, ny)),
            dma((steps, nx)), dma((steps, nx)),
            dma((steps, ny)), dma((steps, ny)),
        ]
        + [pltpu.VMEM((tile_rows + 4 * ghosts, width, tile), BF16) for _ in range(steps)]
        + [pltpu.VMEM((ghosts, width, tile), BF16) for _ in range(steps)]
        + [pltpu.VMEM((ny, piece, s), F32) for s in spans]
        + [pltpu.VMEM((ny, piece, s), F32) for s in spans]
        + [pltpu.VMEM((nx, piece, s), F32) for s in spans]
        + [pltpu.VMEM((ny, piece, s), F32) for s in spans]
        + [pltpu.VMEM((tile_rows, width, tile), BF16)],
        compiler_params=pltpu.CompilerParams(collective_id=0, has_side_effects=True),
    )(send_rows, tile_cols, shifts, start_block, tiles)
    chunk = 2 * tile
    return pl.pallas_call(
        functools.partial(finish_kernel, (steps, width, chunk)),
        out_shape=jax.ShapeDtypeStruct((size, nodes), F32),
        in_specs=[vmem, vmem],
        out_specs=pl.BlockSpec(memory_space=pl.ANY),
        scratch_shapes=[
            pltpu.VMEM((size, size), F32),
            pltpu.VMEM((size, nodes), F32),
            dma((nodes // chunk,)),
        ],
    )(basis, gram)


def solution(mesh):
    in_specs = (
        P(None, ("gx", "gy")),
        P(("gx", "gy"), None, None, None),
        P(("gx", "gy"), None),
        P(("gx", "gy"), None),
        P(),
    )
    out_specs = P(None, ("gx", "gy"))
    run = functools.partial(body, mesh.shape["gx"], mesh.shape["gy"])
    return jax.shard_map(run, mesh=mesh, in_specs=in_specs, out_specs=out_specs, check_vma=False)
```

time: 326 us -> 74.6 us (0.23)
  waiting for transfers between devices: 146 us -> 0 us
  Pallas kernels: 0 us -> 74.4 us
  other arithmetic: 62.1 us -> 0 us
  starting transfers between devices: 53.3 us -> 0 us
  matrix products: 33.4 us -> 0 us
  between operations: 15.3 us -> 0.01 us
  local copies, waits for them, and re-layouts: 14.7 us -> 0 us
    psum x1 -> x0, waiting for transfers between devices: 137 us -> none  [body(): lower = jnp.linalg.cholesky(lax.psum(local_gram, ('gx', 'gy')))]
    pallas_call x0 -> x2, Pallas kernels: none -> 74.4 us  [the longest x1 47.4 us: body(): pl.pallas_call(functools.partial(krylov_kernel, dims), out_shape=(jax.Sha...]
    another operation x10 -> x0, other arithmetic: 55.3 us -> none  [the longest x6 34.1 us: body(): lower = jnp.linalg.cholesky(lax.psum(local_gram, ('gx', 'gy')))]
    ppermute x16 -> x0, starting transfers between devices: 53.3 us -> none  [the longest x8 43 us: extended_2(): lax.ppermute(lax.slice_in_dim(block, block.shape[dim] - width, None, axis...]
    dot_general x5 -> x0, matrix products: 30.3 us -> none  [the longest x4 29.1 us: apply_local(): jnp.einsum('ctkb,tkab->cta', picked, tiles, preferred_element_type=jnp.fl...]
    ppermute x16 -> x0, waiting for transfers between devices: 9.45 us -> none  [the longest x8 8.61 us: extended_2(): lax.ppermute(lax.slice_in_dim(block, block.shape[dim] - width, None, axis...]
    gather x8 -> x0, local copies, waits for them, and re-layouts: 5.19 us -> none  [the longest x4 2.99 us: apply_local(): jnp.take(extended, flat_cols, axis=1).reshape(width, tile_rows, slots, tile)]
    another operation x9 -> x0, local copies, waits for them, and re-layouts: 3.85 us -> none
  transfers between devices with their start and end apart: 17 -> 0, of which waited for: 11 -> 0; matrix products, arithmetic and copies ran while one was open for 1% -> 0% of each run, Pallas kernels for 0% -> 0%
where the time goes in v1:
time: 74.6 us; the launch traced here: 74.4 us
  Pallas kernels  74.4 us (100%)
    pallas_call x1, Pallas kernels, body(): pl.pallas_call(functools.partial(krylov_kernel, dims), out_shape=(jax.Sha...  47.4 us
    pallas_call x1, Pallas kernels, body(): pl.pallas_call(functools.partial(finish_kernel, (steps, width, chunk)), o...  27 us

profile of v1, /device:TPU:0, one launch (start us, length us, event | category | flops | bytes accessed | tf_op | source)
XLA Modules:
  0.0 74.4 jit_solution(3645656164494626644)
XLA Ops:
  0.0 47.4 %shard_map.55 = (bf16[256,2048]{1,0:T(8,128)(2,1)}, f32[256,256]{1,0:T(8,128)}) custom-call(s32[1,2]{1,0:T(1,128)} %send_rows.1, s32[8,10]{1,0:T(8,128)} %tile_cols.1, f32[4]{0:T(128)} %shifts.1, bf16[64,2048]{1,0:T(8,128)(2,1)} %start.1, bf16[8,10,256,256]{3,2,1,0:T(8,128)(2,1)} %tiles_hbm.1), custom_call_target="tpu_custom_call" | custom-call | tf_op jit(solution)/shard_map/pallas_call | solution.py:259
  47.4 27.0 %shard_map.56 = f32[256,2048]{1,0:T(8,128)} custom-call(bf16[256,2048]{1,0:T(8,128)(2,1)} %get-tuple-element.7.basis, f32[256,256]{1,0:T(8,128)} %get-tuple-element.8.gram), custom_call_target="tpu_custom_call" | custom-call | tf_op jit(solution)/shard_map/pallas_call | solution.py:285

commit v2 on v1

--- a/solution.py
+++ b/solution.py
@@ -17,7 +17,7 @@
     return lax.dot_general(a, b, NT_DIMS, precision=precision, preferred_element_type=F32)
 
 
-def krylov_kernel(dims, send_rows, tile_cols, shifts, start, tiles_hbm, basis, gram, *scratch):
+def krylov_kernel(dims, send_rows, tile_cols, shifts, start, tiles_hbm, basis, gram, inverse, *scratch):
     nx, ny, steps, tile_rows, slots, ghosts, tile, width, total = dims
     tiles, tile_sem = scratch[0:2]
     halo_send, halo_recv, rs_send, rs_recv, xs_send, xs_recv, ag_send, ag_recv = scratch[2:10]
@@ -41,6 +41,7 @@
     for s in range(steps):
         ext[s][tile_rows:] = jnp.zeros(ext[s][tile_rows:].shape, BF16)
 
+    inverse[...] = jnp.zeros(inverse.shape, F32)
     barrier = pltpu.get_barrier_semaphore()
 
     def greet_y(d, c):
@@ -141,8 +142,10 @@
     def phase_4(u):
         each(ny, lambda d: ag_copy(u, d).wait_recv())
         for p in range(ny):
-            low = u * width + p * piece
+            low = p * piece
             gram[low:low + piece, :full[u].shape[2]] = full[u][p]
+        if u + 1 < steps:
+            extend_inverse(u, width, gram[:, :(u + 1) * width], inverse)
 
     def drain(u):
         each(ny, lambda d: rs_copy(u, d).wait_send())
@@ -165,6 +168,8 @@
             for s in range(ghosts):
                 outbox[j + 1][s] = row_image(j, send_rows[0, s])
             halo_start(j + 1)
+        if j >= 1:
+            phase_2(j - 1)
 
         def row(t, c):
             value = row_image(j, t)
@@ -179,55 +184,72 @@
             part[j][p] = local[p * piece:(p + 1) * piece]
         phase_1(j)
         if j >= 1:
-            phase_2(j - 1)
-        if j >= 2:
-            phase_3(j - 2)
+            phase_3(j - 1)
+        if 2 <= j < steps - 1:
+            phase_4(j - 2)
 
     last = steps - 1
-    phase_2(last)
-    if steps > 1:
-        phase_3(last - 1)
-    phase_3(last)
-    for u in range(steps):
+    waiting = list(range(max(0, last - 2), last))
+    for act in (phase_2, phase_3):
+        if waiting:
+            phase_4(waiting.pop(0))
+        act(last)
+    for u in waiting + [last]:
         phase_4(u)
     for u in range(steps):
         halo_drain(u)
         drain(u)
 
 
-def finish_kernel(dims, basis, gram, out, inverse, staged, sem):
-    steps, width, chunk = dims
-    high = lax.Precision.HIGHEST
-    size = steps * width
-    inverse[...] = jnp.zeros((size, size), F32)
-    rows = lax.broadcasted_iota(jnp.int32, (8, 2 * width), 0)
+def factor(block):
+    width = block.shape[0]
+    count = width // 8
     eye_r = lax.broadcasted_iota(jnp.int32, (width, width), 0)
     eye_c = lax.broadcasted_iota(jnp.int32, (width, width), 1)
-    eye = jnp.where(eye_r == eye_c, 1.0, 0.0).astype(F32)
-    for j in range(steps):
-        lo, hi = j * width, (j + 1) * width
-        block = gram[lo:hi, lo:hi]
-        if j:
-            previous = inverse[0:lo, 0:lo]
-            left = nt(gram[lo:hi, 0:lo], previous, high)
-            block = block - nt(left, left, high)
-        work = jnp.concatenate([block, eye], axis=1)
-        groups = [work[g * 8:(g + 1) * 8] for g in range(width // 8)]
-        done = []
-        for k in range(width):
-            g, r = k // 8, k % 8
-            pivot_row = groups[g][r:r + 1]
-            pivot = groups[g][r:r + 1, k:k + 1]
-            done.append(pivot_row * lax.rsqrt(pivot))
-            scaled = pivot_row / pivot
-            for h in range(g, width // 8):
-                update = groups[h] - groups[h][:, k:k + 1] * scaled
+    work = jnp.concatenate([block, jnp.where(eye_r == eye_c, 1.0, 0.0).astype(F32)], axis=1)
+    rows = lax.broadcasted_iota(jnp.int32, (8, 2 * width), 0)
+    groups = [work[g * 8:(g + 1) * 8] for g in range(count)]
+    done = []
+    for g in range(count):
+        cols = [
+            [jnp.broadcast_to(groups[h][:, g * 8 + r:g * 8 + r + 1], (8, 2 * width)) for h in range(g, count)]
+            for r in range(8)
+        ]
+        pivots = cols[0][0]
+        for r in range(8):
+            inverse = 1.0 / cols[r][0][r:r + 1]
+            if r:
+                pivots = jnp.where(rows == r, cols[r][0], pivots)
+            for m in range(r + 1, 8):
+                share = cols[m][0][r:r + 1] * inverse
+                cols[m] = [c - d * share for c, d in zip(cols[m], cols[r])]
+            scaled = groups[g][r:r + 1] * inverse
+            for h in range(g, count):
+                update = groups[h] - cols[r][h - g] * scaled
                 groups[h] = jnp.where(rows > r, update, groups[h]) if h == g else update
-        own = jnp.concatenate(done, axis=0)[:, width:]
-        inverse[lo:hi, lo:hi] = own
-        if j:
-            cross = jnp.dot(left, previous, precision=high, preferred_element_type=F32)
-            inverse[lo:hi, 0:lo] = -jnp.dot(own, cross, precision=high, preferred_element_type=F32)
+        done.append(groups[g] * lax.rsqrt(pivots))
+    return jnp.concatenate(done, axis=0)[:, width:]
+
+
+def extend_inverse(j, width, gram_row, inverse):
+    high = lax.Precision.HIGHEST
+    lo, hi = j * width, (j + 1) * width
+    block = gram_row[:, lo:hi]
+    if j:
+        previous = inverse[0:lo, 0:lo]
+        left = nt(gram_row[:, 0:lo], previous, high)
+        block = block - nt(left, left, high)
+    own = factor(block)
+    inverse[lo:hi, lo:hi] = own
+    if j:
+        cross = jnp.dot(left, previous, precision=high, preferred_element_type=F32)
+        inverse[lo:hi, 0:lo] = -jnp.dot(own, cross, precision=high, preferred_element_type=F32)
+
+
+def finish_kernel(dims, basis, gram, above, out, inverse, staged, sem):
+    steps, width, chunk = dims
+    inverse[...] = above[...]
+    extend_inverse(steps - 1, width, gram[...], inverse)
     whole = inverse[...]
     main = whole.astype(BF16)
     rest = (whole - main.astype(F32)).astype(BF16)
@@ -256,14 +278,15 @@
     dma = pltpu.SemaphoreType.DMA
     vmem = pl.BlockSpec(memory_space=pltpu.VMEM)
     smem = pl.BlockSpec(memory_space=pltpu.SMEM)
-    basis, gram = pl.pallas_call(
+    basis, gram, above = pl.pallas_call(
         functools.partial(krylov_kernel, dims),
         out_shape=(
             jax.ShapeDtypeStruct((size, nodes), BF16),
+            jax.ShapeDtypeStruct((width, spans[-1]), F32),
             jax.ShapeDtypeStruct((size, size), F32),
         ),
         in_specs=[smem, smem, smem, vmem, pl.BlockSpec(memory_space=pl.ANY)],
-        out_specs=(vmem, vmem),
+        out_specs=(vmem, vmem, vmem),
         scratch_shapes=[
             pltpu.VMEM(tiles.shape, BF16),
             dma((tile_rows,)),
@@ -285,14 +308,14 @@
     return pl.pallas_call(
         functools.partial(finish_kernel, (steps, width, chunk)),
         out_shape=jax.ShapeDtypeStruct((size, nodes), F32),
-        in_specs=[vmem, vmem],
+        in_specs=[vmem, vmem, vmem],
         out_specs=pl.BlockSpec(memory_space=pl.ANY),
         scratch_shapes=[
             pltpu.VMEM((size, size), F32),
             pltpu.VMEM((size, nodes), F32),
             dma((nodes // chunk,)),
         ],
-    )(basis, gram)
+    )(basis, gram, above)
 
 
 def solution(mesh):

time: 74.6 us -> 61.4 us (0.82)
  Pallas kernels: 74.4 us -> 61.3 us
    pallas_call x1, Pallas kernels: 27 us -> 5.48 us  [body(): pl.pallas_call(functools.partial(finish_kernel, (steps, width, chunk)), o...]
    pallas_call x1, Pallas kernels: 47.4 us -> 55.8 us  [body(): pl.pallas_call(functools.partial(krylov_kernel, dims), out_shape=(jax.Sha...]
where the time goes in v2:
time: 61.4 us; the launch traced here: 61.3 us
  Pallas kernels  61.3 us (100%)
    pallas_call x1, Pallas kernels, body(): pl.pallas_call(functools.partial(krylov_kernel, dims), out_shape=(jax.Sha...  55.8 us
    pallas_call x1, Pallas kernels, body(): pl.pallas_call(functools.partial(finish_kernel, (steps, width, chunk)), o...  5.48 us

profile of v2, /device:TPU:0, one launch (start us, length us, event | category | flops | bytes accessed | tf_op | source)
XLA Modules:
  0.0 61.3 jit_solution(10752720647542936908)
XLA Ops:
  0.0 55.8 %shard_map.55 = (bf16[256,2048]{1,0:T(8,128)(2,1)}, f32[64,256]{1,0:T(8,128)}, f32[256,256]{1,0:T(8,128)}) custom-call(s32[1,2]{1,0:T(1,128)} %send_rows.1, s32[8,10]{1,0:T(8,128)} %tile_cols.1, f32[4]{0:T(128)} %shifts.1, bf16[64,2048]{1,0:T(8,128)(2,1)} %start.1, bf16[8,10,256,256]{3,2,1,0:T(8,128)(2,1)} %tiles_hbm.1), custom_call_target="tpu_custom_call" | custom-call | tf_op jit(solution)/shard_map/pallas_call | solution.py:281
  55.8 5.5 %shard_map.56 = f32[256,2048]{1,0:T(8,128)} custom-call(bf16[256,2048]{1,0:T(8,128)(2,1)} %get-tuple-element.8.basis, f32[64,256]{1,0:T(8,128)} %get-tuple-element.9.gram, f32[256,256]{1,0:T(8,128)} %get-tuple-element.10.above), custom_call_target="tpu_custom_call" | custom-call | tf_op jit(solution)/shard_map/pallas_call | solution.py:308

commit v3 on v2

--- a/solution.py
+++ b/solution.py
@@ -153,14 +153,20 @@
         each(ny, lambda d: ag_copy(u, d).wait_send())
 
     def row_image(j, r):
-        acc = nt(ext[j][tile_cols[r, 0]], tiles[r, 0])
+        acc = jnp.dot(ext[j][tile_cols[r, 0]], tiles[r, 0], preferred_element_type=F32)
         for k in range(1, slots):
-            acc = acc + nt(ext[j][tile_cols[r, k]], tiles[r, k])
+            acc = acc + jnp.dot(ext[j][tile_cols[r, k]], tiles[r, k], preferred_element_type=F32)
         return (acc - shifts[j] * ext[j][r].astype(F32)).astype(BF16)
 
     halo_start(0)
-    for t in range(tile_rows):
+
+    def turned(t, c):
         tile_copy(t).wait()
+        for k in range(slots):
+            tiles[t, k] = tiles[t, k].T
+        return c
+
+    lax.fori_loop(0, tile_rows, turned, 0)
 
     for j in range(steps):
         halo_wait(j)
@@ -178,7 +184,7 @@
             basis[j * width:(j + 1) * width, pl.ds(pl.multiple_of(t * tile, tile), tile)] = value
             return c
 
-        lax.fori_loop(0, tile_rows, row, 0)
+        lax.fori_loop(0, tile_rows, row, 0, unroll=4)
         local = nt(basis[j * width:(j + 1) * width, :], basis[0:part[j].shape[2], :]) / total
         for p in range(ny):
             part[j][p] = local[p * piece:(p + 1) * piece]

time: 61.4 us -> 52.6 us (0.86)
  Pallas kernels: 61.3 us -> 52.4 us
    pallas_call x1, Pallas kernels: 55.8 us -> 46.9 us  [body(): pl.pallas_call(functools.partial(krylov_kernel, dims), out_shape=(jax.Sha...]
where the time goes in v3:
time: 52.6 us; the launch traced here: 52.4 us
  Pallas kernels  52.4 us (100%)
    pallas_call x1, Pallas kernels, body(): pl.pallas_call(functools.partial(krylov_kernel, dims), out_shape=(jax.Sha...  46.9 us
    pallas_call x1, Pallas kernels, body(): pl.pallas_call(functools.partial(finish_kernel, (steps, width, chunk)), o...  5.48 us

profile of v3, /device:TPU:0, one launch (start us, length us, event | category | flops | bytes accessed | tf_op | source)
XLA Modules:
  0.0 52.4 jit_solution(10569727642808082281)
XLA Ops:
  0.0 46.9 %shard_map.55 = (bf16[256,2048]{1,0:T(8,128)(2,1)}, f32[64,256]{1,0:T(8,128)}, f32[256,256]{1,0:T(8,128)}) custom-call(s32[1,2]{1,0:T(1,128)} %send_rows.1, s32[8,10]{1,0:T(8,128)} %tile_cols.1, f32[4]{0:T(128)} %shifts.1, bf16[64,2048]{1,0:T(8,128)(2,1)} %start.1, bf16[8,10,256,256]{3,2,1,0:T(8,128)(2,1)} %tiles_hbm.1), custom_call_target="tpu_custom_call" | custom-call | tf_op jit(solution)/shard_map/pallas_call | solution.py:287
  46.9 5.5 %shard_map.56 = f32[256,2048]{1,0:T(8,128)} custom-call(bf16[256,2048]{1,0:T(8,128)(2,1)} %get-tuple-element.8.basis, f32[64,256]{1,0:T(8,128)} %get-tuple-element.9.gram, f32[256,256]{1,0:T(8,128)} %get-tuple-element.10.above), custom_call_target="tpu_custom_call" | custom-call | tf_op jit(solution)/shard_map/pallas_call | solution.py:314
